TPU v7x, 32 devices: a whole 2x2x4 slice. The times are simulated.
32 devices in a mesh: seq: 4 (over y, core), head: 8 (over z, x).
Axes of the slice: x: 2, y: 2, z: 4, core: 2. Of those that a mesh axis runs over, the one named last changes fastest.
Arguments:
- query_rows: bfloat16 [4096, 8192], P(('seq', 'head')), may hold values from -6 to 6
- key_rows: bfloat16 [4096, 1024], P(('seq', 'head')), may hold values from -6 to 6
- value_rows: bfloat16 [4096, 1024], P(('seq', 'head')), may hold values from -6 to 6
- grad_out: bfloat16 [8192, 8192], P(('seq', 'head')), may hold values from -6 to 6
- doc_ids: int32 [32], replicated, may hold values from 0 to 7, never falling along the last dimension, each value on 1 to 7 neighbouring positions
- route_table: int32 [4, 4, 4], replicated, may hold values from 0 to 8, as said below
Outputs:
- attn_out: bfloat16 [8192, 8192], P(('seq', 'head'))
- grad_query: bfloat16 [4096, 8192], P(('seq', 'head'))
- grad_key: bfloat16 [4096, 1024], P(('seq', 'head'))
- grad_value: bfloat16 [4096, 1024], P(('seq', 'head'))
Inputs may be any that keep to these rules, and one draw needn't show every extreme that they name: route_table[s, t, c] is a block of sequence shard s (numbered within the shard) that seq index t takes into slot c, or 8 for an empty slot; every block of every shard appears exactly once; live slots come first in each (s, t) row; each shard fills all 4 slots for a quarter of the seq indices, 2 slots for half of them and none for the rest; one seq index has every slot live.
All inputs are finite; a program needn't handle non-finite values.
Results may differ from a plain program's by a relative error of at most 0.015.
Values may be sent and summed in bfloat16 or wider, within the bound.
No kernel may reach another device: no remote copies, remote signals or barrier semaphores. Data moves between devices by JAX's collectives and lax.ppermute only.
A program may use at most 192 MiB of HBM per device.

v0:
```python
import math
import jax
import jax.numpy as jnp
from jax import lax
from jax.sharding import PartitionSpec as P

QH = 64
KVH = 8
DH = 128
BLOCK = 128
DOCMAX = 7


def slot_pass(queries, cotangent, keys_win, values_win, allowed, alive_flag, factor):
    scores = (
        jnp.einsum("bpd,nd->pbn", queries, keys_win, preferred_element_type=jnp.float32) * factor
    )
    scores = jnp.where(allowed[None], scores, -jnp.inf)
    rowmax = jnp.max(scores, axis=-1, keepdims=True)
    exponent = jnp.where(allowed[None], jnp.exp(scores - rowmax), jnp.zeros_like(scores))
    weights = exponent / jnp.sum(exponent, axis=-1, keepdims=True)
    weights_b = weights.astype(jnp.bfloat16)
    output = jnp.einsum("pbn,nd->bpd", weights_b, values_win, preferred_element_type=jnp.float32)
    output = jnp.where(alive_flag, output, jnp.zeros_like(output)).astype(jnp.bfloat16)
    cotangent = jnp.where(alive_flag, cotangent, jnp.zeros_like(cotangent))
    deltas = jnp.sum(cotangent.astype(jnp.float32) * output.astype(jnp.float32), axis=-1)
    prob_grad = jnp.einsum("bpd,nd->pbn", cotangent, values_win, preferred_element_type=jnp.float32)
    dscore = (weights * (prob_grad - deltas.T[:, :, None]) * factor).astype(jnp.bfloat16)
    grad_rows = jnp.einsum(
        "pbn,nd->bpd", dscore, keys_win, preferred_element_type=jnp.float32
    ).astype(jnp.bfloat16)
    key_part = jnp.einsum("pbn,bpd->nd", dscore, queries, preferred_element_type=jnp.float32)
    value_part = jnp.einsum("pbn,bpd->nd", weights_b, cotangent, preferred_element_type=jnp.float32)
    return (output, grad_rows, jnp.concatenate([key_part, value_part], axis=-1))


def body(query_rows, key_rows, value_rows, grad_out, doc_ids, route_table):
    tok_count = query_rows.shape[0]
    heads_axis = lax.axis_size("head")
    seq_count = lax.axis_size("seq")
    per_dev = QH // heads_axis
    repeats = heads_axis // KVH
    blocks_shard = tok_count * heads_axis // BLOCK
    slot_cap = route_table.shape[2]
    slot_total = seq_count * slot_cap
    total_tok = tok_count * heads_axis * seq_count
    window = DOCMAX * BLOCK
    margin = (DOCMAX - 1) * BLOCK
    factor = 1.0 / math.sqrt(DH)
    query_split = query_rows.reshape(tok_count, heads_axis, per_dev * DH)
    key_value = jnp.concatenate(
        [key_rows.reshape(tok_count, KVH, 1, DH), value_rows.reshape(tok_count, KVH, 1, DH)],
        axis=-1,
    )
    key_value = jnp.broadcast_to(key_value, (tok_count, KVH, repeats, 2 * DH)).reshape(
        tok_count, heads_axis, 2 * DH
    )
    query_local, pairs_local = (
        lax.all_to_all(query_split, "head", split_axis=1, concat_axis=0, tiled=True),
        lax.all_to_all(key_value, "head", split_axis=1, concat_axis=0, tiled=True),
    )
    pairs_all = lax.all_gather(pairs_local, "seq", axis=0, tiled=True).reshape(total_tok, 2 * DH)
    grad_split = grad_out.reshape(2 * tok_count, heads_axis, per_dev * DH)
    grad_local = lax.all_to_all(
        grad_split, "head", split_axis=1, concat_axis=0, tiled=True
    ).reshape(slot_total, BLOCK, per_dev, DH)
    seq_self = lax.axis_index("seq")
    send_index = lax.dynamic_index_in_dim(route_table, seq_self, 0, keepdims=False)
    send_live = send_index < blocks_shard
    send_safe = jnp.where(send_live, send_index, 0)
    query_blocks = query_local.reshape(blocks_shard, BLOCK, per_dev * DH)
    outgoing = jnp.take(query_blocks, send_safe.reshape(-1), axis=0).reshape(
        seq_count, slot_cap, BLOCK, per_dev * DH
    )
    incoming = lax.all_to_all(outgoing, "seq", split_axis=0, concat_axis=0, tiled=True).reshape(
        slot_total, BLOCK, per_dev, DH
    )
    recv_index = lax.dynamic_index_in_dim(route_table, seq_self, 1, keepdims=False).reshape(-1)
    alive_slot = recv_index < blocks_shard
    source = jnp.repeat(jnp.arange(seq_count, dtype=jnp.int32), slot_cap)
    block_ids = jnp.where(alive_slot, source * blocks_shard + recv_index, 0)
    pairs_pad = jnp.concatenate([jnp.zeros((margin, 2 * DH), jnp.bfloat16), pairs_all], axis=0)
    doc_pad = jnp.concatenate([jnp.full((DOCMAX - 1,), -1, jnp.int32), doc_ids])
    columns = jnp.arange(window)
    row_pos = jnp.arange(BLOCK)
    causal = (columns[None, :] < margin) | (columns[None, :] - margin <= row_pos[:, None])
    group_size = 4
    group_count = slot_total // group_size

    def one_slot(queries, cotangent, block_id, alive_flag):
        pairs_win = lax.dynamic_slice_in_dim(pairs_pad, block_id * BLOCK, window, 0)
        docs_win = lax.dynamic_slice_in_dim(doc_pad, block_id, DOCMAX, 0)
        same_doc = jnp.repeat(docs_win == docs_win[DOCMAX - 1], BLOCK)
        allowed = causal & same_doc[None, :]
        return slot_pass(
            queries, cotangent, pairs_win[:, :DH], pairs_win[:, DH:], allowed, alive_flag, factor
        )

    def group_step(partial_value, group_index):
        first_slot = group_index * group_size
        queries = lax.dynamic_slice_in_dim(incoming, first_slot, group_size, 0)
        cotangent = lax.dynamic_slice_in_dim(grad_local, first_slot, group_size, 0)
        slot_ids = lax.dynamic_slice_in_dim(block_ids, first_slot, group_size, 0)
        alive_flags = lax.dynamic_slice_in_dim(alive_slot, first_slot, group_size, 0)
        outputs, grad_rows, updates = jax.vmap(one_slot)(queries, cotangent, slot_ids, alive_flags)
        for member in range(group_size):
            row_start = slot_ids[member] * BLOCK
            current = lax.dynamic_slice_in_dim(partial_value, row_start, window, 0)
            partial_value = lax.dynamic_update_slice_in_dim(
                partial_value, current + updates[member], row_start, 0
            )
        return (partial_value, (outputs, grad_rows))

    partial_init = jnp.zeros((margin + total_tok, 2 * DH), jnp.float32)
    partial_value, (outputs, grad_rows) = lax.scan(
        group_step, partial_init, jnp.arange(group_count)
    )
    out_slots = outputs.reshape(slot_total * BLOCK, 1, per_dev * DH)
    attn_out = lax.all_to_all(out_slots, "head", split_axis=0, concat_axis=1, tiled=True).reshape(
        2 * tok_count, QH * DH
    )
    back_slots = grad_rows.reshape(seq_count, slot_cap, BLOCK, per_dev * DH)
    returned = lax.all_to_all(back_slots, "seq", split_axis=0, concat_axis=0, tiled=True).reshape(
        slot_total, BLOCK, per_dev * DH
    )
    place_idx = jnp.where(send_live, send_index, blocks_shard).reshape(-1)
    own_blocks = (
        jnp.zeros((blocks_shard + 1, BLOCK, per_dev * DH), jnp.bfloat16).at[place_idx].set(returned)
    )
    own_rows = own_blocks[:blocks_shard].reshape(blocks_shard * BLOCK, 1, per_dev * DH)
    grad_query = lax.all_to_all(own_rows, "head", split_axis=0, concat_axis=1, tiled=True).reshape(
        tok_count, QH * DH
    )
    summed_rows = lax.psum_scatter(
        partial_value[margin:].astype(jnp.bfloat16), "seq", scatter_dimension=0, tiled=True
    )
    summed_rows = summed_rows.reshape(blocks_shard * BLOCK, 1, 2 * DH)
    spread = lax.all_to_all(summed_rows, "head", split_axis=0, concat_axis=1, tiled=True)
    merged = jnp.sum(
        spread.reshape(tok_count, KVH, repeats, 2 * DH).astype(jnp.float32), axis=2
    ).astype(jnp.bfloat16)
    grad_key = merged[:, :, :DH].reshape(tok_count, KVH * DH)
    grad_value = merged[:, :, DH:].reshape(tok_count, KVH * DH)
    return (attn_out, grad_query, grad_key, grad_value)


def solution(mesh):
    in_specs = (
        P(("seq", "head"), None),
        P(("seq", "head"), None),
        P(("seq", "head"), None),
        P(("seq", "head"), None),
        P(),
        P(),
    )
    out_specs = (
        P(("seq", "head"), None),
        P(("seq", "head"), None),
        P(("seq", "head"), None),
        P(("seq", "head"), None),
    )
    return jax.shard_map(body, mesh=mesh, in_specs=in_specs, out_specs=out_specs, check_vma=False)
```

profile of v0, /device:TPU:0, one launch (start us, length us, event | category | flops | bytes accessed | tf_op | source)
XLA Modules:
  0.0 827.7 jit_solution(8605407508596196306)
XLA Ops:
  23.2 8.7 %all-to-all-done = bf16[128,8,256]{2,0,1:T(8,128)(2,1)S(1)} async-done(((bf16[128,8,256]{2,0,1:T(8,128)(2,1)}), bf16[128,8,256]{2,0,1:T(8,128)(2,1)S(1)}, u32[]{:S(2)}, u32[]{:S(2)}) %all-to-all-start) | async-done | bytes 524320 | tf_op jit(solution)/shard_map/all_to_all | solution.py:60
  40.3 43.6 %all-to-all-done.1 = bf16[128,8,1024]{2,0,1:T(8,128)(2,1)S(1)} async-done(((bf16[128,8,1024]{2,0,1:T(8,128)(2,1)}), bf16[128,8,1024]{2,0,1:T(8,128)(2,1)S(1)}, u32[]{:S(2)}, u32[]{:S(2)}) %all-to-all-start.1) | async-done | bytes 2097184 | tf_op jit(solution)/shard_map/all_to_all | solution.py:59
  103.4 77.7 %all-to-all-done.3 = bf16[256,8,1024]{2,0,1:T(8,128)(2,1)} async-done(((bf16[256,8,1024]{2,0,1:T(8,128)(2,1)}), bf16[256,8,1024]{2,0,1:T(8,128)(2,1)}, u32[]{:S(2)}, u32[]{:S(2)}) %all-to-all-start.3) | async-done | bytes 4194336 | tf_op jit(solution)/shard_map/all_to_all | solution.py:64
  194.9 39.3 %all-to-all-done.2 = bf16[4,4,128,1024]{2,3,1,0:T(8,128)(2,1)} async-done(((bf16[4,4,128,1024]{2,3,1,0:T(8,128)(2,1)}), bf16[4,4,128,1024]{2,3,1,0:T(8,128)(2,1)}, u32[]{:S(2)}, u32[]{:S(2)}) %all-to-all-start.2) | async-done | bytes 4194336 | tf_op jit(solution)/shard_map/all_to_all | solution.py:75
  236.8 298.6 %while.23 = (s32[]{:T(128)}, f32[4864,256]{0,1:T(8,128)}, bf16[4,4,128,8,128]{4,3,2,1,0:T(8,128)(2,1)}, bf16[4,4,128,8,128]{2,4,3,1,0:T(8,128)(2,1)}, s32[4]{0:T...) while((s32[]{:T(128)}, f32[4864,256]{0,1:T(8,128)}, ...), condition=%wide.region_4.5_spmd.clone, body=%wide.region_0.0_spmd.clone.sunk | while | flops 5688947712 | bytes 244061568 | solution.py:115
  250.2 9.5 %while.25 = (s32[]{:T(128)}, bf16[4864,256]{1,0:T(8,128)(2,1)}, s32[4,2]{0,1:T(2,128)S(1)}, bf16[4,896,256]{2,1,0:T(8,128)(2,1)S(1)}, s32[]{:T(128)}) while((s32[]{:T(128)}, bf16[4864,256]{1,0:T(8,128)(2,1)}, s32[4,2]{0,1:T(2,128)S(1)}, bf16[4,896,256]{2,1,0:T(8,128)(2,1)S(1)}, s32[]{:T(128)}) %tuple.86), condition=%wide.while_cond.1, body=%wide.while_body.1.sunk | while | flops 2 | bytes 917609 | solution.py:91
  259.8 10.0 %fusion.113 = (f32[4,8,128]{2,1,0:T(8,128)S(1)}, f32[4,8,128,896]{2,3,1,0:T(8,128)}) fusion(pred[4,128,896]{1,2,0:T(8,128)(4,1)S(1)} %broadcast_and_fusion.2, bf16[16,128,8,128]{1,3,2,0:T(8,128)(2,1)} %get-tuple-element.513, s32[]{:T(128)S(6)} %select_n.197, bf16[4,896,256]{2,1,0:T(8,128)(2,1)S(1)} %get-tuple-element.411), kind=kOutput, calls=%fused_computation.105.clone.1 | convolution fusion | flops 957875072 | bytes 17580036 | tf_op jit(solution)/shard_map/while/body/eval_jaxpr/vmap()/sub | solution.py:20
  269.8 9.9 %fusion.114 = bf16[4,8,128,896]{2,3,1,0:T(8,128)(2,1)} fusion(f32[4,8,128,896]{2,3,1,0:T(8,128)} %get-tuple-element.412, f32[4,8,128]{2,1,0:T(8,128)S(1)} %get-tuple-element.413), kind=kLoop, calls=%fused_computation.19.clone.1 | loop fusion | flops 7340032 | bytes 22036480 | tf_op jit(solution)/shard_map/while/body/eval_jaxpr/vmap()/convert_element_type | solution.py:22
  287.7 8.5 %fusion.115 = bf16[4,8,128,896]{2,3,1,0:T(8,128)(2,1)} fusion(f32[4,8,128]{2,1,0:T(8,128)S(1)} %bitcast.276, f32[4,8,128,896]{2,3,1,0:T(8,128)} %get-tuple-element.412, f32[4,8,128]{2,1,0:T(8,128)S(1)} %get-tuple-element.413, bf16[4,896,256]{2,1,0:T(8,128)(2,1)S(1)} %copy-done.4, bf16[4,128,8,128]{1,3,2,0:T(8,128)(2,1)S(1)} %copy.188, ...), kind=kOutput, calls=%fused_computation.11.clone.1 | convolution fusion | flops 958398464 | bytes 24019456 | tf_op jit(solution)/shard_map/while/body/eval_jaxpr/vmap(bpd,nd->pbn)/dot_general | solution.py:27
  324.9 9.5 %while.25 = (s32[]{:T(128)}, bf16[4864,256]{1,0:T(8,128)(2,1)}, s32[4,2]{0,1:T(2,128)S(1)}, bf16[4,896,256]{2,1,0:T(8,128)(2,1)S(1)}, s32[]{:T(128)}) while((s32[]{:T(128)}, bf16[4864,256]{1,0:T(8,128)(2,1)}, s32[4,2]{0,1:T(2,128)S(1)}, bf16[4,896,256]{2,1,0:T(8,128)(2,1)S(1)}, s32[]{:T(128)}) %tuple.86), condition=%wide.while_cond.1, body=%wide.while_body.1.sunk | while | flops 2 | bytes 917609 | solution.py:91
  334.5 10.0 %fusion.113 = (f32[4,8,128]{2,1,0:T(8,128)S(1)}, f32[4,8,128,896]{2,3,1,0:T(8,128)}) fusion(pred[4,128,896]{1,2,0:T(8,128)(4,1)S(1)} %broadcast_and_fusion.2, bf16[16,128,8,128]{1,3,2,0:T(8,128)(2,1)} %get-tuple-element.513, s32[]{:T(128)S(6)} %select_n.197, bf16[4,896,256]{2,1,0:T(8,128)(2,1)S(1)} %get-tuple-element.411), kind=kOutput, calls=%fused_computation.105.clone.1 | convolution fusion | flops 957875072 | bytes 17580036 | tf_op jit(solution)/shard_map/while/body/eval_jaxpr/vmap()/sub | solution.py:20
  344.4 9.9 %fusion.114 = bf16[4,8,128,896]{2,3,1,0:T(8,128)(2,1)} fusion(f32[4,8,128,896]{2,3,1,0:T(8,128)} %get-tuple-element.412, f32[4,8,128]{2,1,0:T(8,128)S(1)} %get-tuple-element.413), kind=kLoop, calls=%fused_computation.19.clone.1 | loop fusion | flops 7340032 | bytes 22036480 | tf_op jit(solution)/shard_map/while/body/eval_jaxpr/vmap()/convert_element_type | solution.py:22
  399.6 9.5 %while.25 = (s32[]{:T(128)}, bf16[4864,256]{1,0:T(8,128)(2,1)}, s32[4,2]{0,1:T(2,128)S(1)}, bf16[4,896,256]{2,1,0:T(8,128)(2,1)S(1)}, s32[]{:T(128)}) while((s32[]{:T(128)}, bf16[4864,256]{1,0:T(8,128)(2,1)}, s32[4,2]{0,1:T(2,128)S(1)}, bf16[4,896,256]{2,1,0:T(8,128)(2,1)S(1)}, s32[]{:T(128)}) %tuple.86), condition=%wide.while_cond.1, body=%wide.while_body.1.sunk | while | flops 2 | bytes 917609 | solution.py:91
  409.2 10.0 %fusion.113 = (f32[4,8,128]{2,1,0:T(8,128)S(1)}, f32[4,8,128,896]{2,3,1,0:T(8,128)}) fusion(pred[4,128,896]{1,2,0:T(8,128)(4,1)S(1)} %broadcast_and_fusion.2, bf16[16,128,8,128]{1,3,2,0:T(8,128)(2,1)} %get-tuple-element.513, s32[]{:T(128)S(6)} %select_n.197, bf16[4,896,256]{2,1,0:T(8,128)(2,1)S(1)} %get-tuple-element.411), kind=kOutput, calls=%fused_computation.105.clone.1 | convolution fusion | flops 957875072 | bytes 17580036 | tf_op jit(solution)/shard_map/while/body/eval_jaxpr/vmap()/sub | solution.py:20
  419.1 9.9 %fusion.114 = bf16[4,8,128,896]{2,3,1,0:T(8,128)(2,1)} fusion(f32[4,8,128,896]{2,3,1,0:T(8,128)} %get-tuple-element.412, f32[4,8,128]{2,1,0:T(8,128)S(1)} %get-tuple-element.413), kind=kLoop, calls=%fused_computation.19.clone.1 | loop fusion | flops 7340032 | bytes 22036480 | tf_op jit(solution)/shard_map/while/body/eval_jaxpr/vmap()/convert_element_type | solution.py:22
  474.2 9.5 %while.25 = (s32[]{:T(128)}, bf16[4864,256]{1,0:T(8,128)(2,1)}, s32[4,2]{0,1:T(2,128)S(1)}, bf16[4,896,256]{2,1,0:T(8,128)(2,1)S(1)}, s32[]{:T(128)}) while((s32[]{:T(128)}, bf16[4864,256]{1,0:T(8,128)(2,1)}, s32[4,2]{0,1:T(2,128)S(1)}, bf16[4,896,256]{2,1,0:T(8,128)(2,1)S(1)}, s32[]{:T(128)}) %tuple.86), condition=%wide.while_cond.1, body=%wide.while_body.1.sunk | while | flops 2 | bytes 917609 | solution.py:91
  483.8 10.0 %fusion.113 = (f32[4,8,128]{2,1,0:T(8,128)S(1)}, f32[4,8,128,896]{2,3,1,0:T(8,128)}) fusion(pred[4,128,896]{1,2,0:T(8,128)(4,1)S(1)} %broadcast_and_fusion.2, bf16[16,128,8,128]{1,3,2,0:T(8,128)(2,1)} %get-tuple-element.513, s32[]{:T(128)S(6)} %select_n.197, bf16[4,896,256]{2,1,0:T(8,128)(2,1)S(1)} %get-tuple-element.411), kind=kOutput, calls=%fused_computation.105.clone.1 | convolution fusion | flops 957875072 | bytes 17580036 | tf_op jit(solution)/shard_map/while/body/eval_jaxpr/vmap()/sub | solution.py:20
  493.8 9.9 %fusion.114 = bf16[4,8,128,896]{2,3,1,0:T(8,128)(2,1)} fusion(f32[4,8,128,896]{2,3,1,0:T(8,128)} %get-tuple-element.412, f32[4,8,128]{2,1,0:T(8,128)S(1)} %get-tuple-element.413), kind=kLoop, calls=%fused_computation.19.clone.1 | loop fusion | flops 7340032 | bytes 22036480 | tf_op jit(solution)/shard_map/while/body/eval_jaxpr/vmap()/convert_element_type | solution.py:22
  545.5 36.1 %reduce-scatter.2.cloned.1.call-done = bf16[1024,256]{1,0:T(8,128)(2,1)} async-done(((bf16[4096,256]{1,0:T(8,128)(2,1)}), bf16[1024,256]{1,0:T(8,128)(2,1)}) %reduce-scatter.2.cloned.1.call-update) | async-done | bytes 524304 | tf_op jit(solution)/shard_map/reduce_scatter | solution.py:134
  585.1 19.8 %all-to-all-done.5 = bf16[4,4,128,1024]{2,3,1,0:T(8,128)(2,1)} async-done(((bf16[4,4,128,1024]{2,3,1,0:T(8,128)(2,1)}), bf16[4,4,128,1024]{2,3,1,0:T(8,128)(2,1)}, u32[]{:S(2)}, u32[]{:S(2)}) %all-to-all-start.5) | async-done | bytes 4194336 | tf_op jit(solution)/shard_map/all_to_all | solution.py:123
  636.5 23.8 %reshape.247 = bf16[2048,1,1024]{2,1,0:T(2,128)(2,1)} reshape(bf16[4,4,128,8,128]{4,3,2,1,0:T(8,128)(2,1)} %get-tuple-element.68) | data formatting | bytes 8388608 | tf_op jit(solution)/shard_map/reshape | solution.py:118
  660.4 26.0 %reduce.6 = bf16[2048,1024]{1,0:T(8,128)(2,1)} reduce(bf16[2048,1,1024]{2,1,0:T(2,128)(2,1)} %reshape.247, bf16[]{:T(256)} %broadcast.238), dimensions={1}, to_apply=%reshape.247.reduce_sub_computation | reduce | bytes 8388610 | tf_op jit(solution)/shard_map/reshape | solution.py:118
  718.5 73.7 %all-to-all-done.4 = bf16[8,2,131072]{2,1,0:T(2,128)(2,1)} async-done(((bf16[8,2,131072]{2,1,0:T(2,128)(2,1)}), bf16[8,2,131072]{2,1,0:T(2,128)(2,1)}, u32[]{:S(2)}, u32[]{:S(2)}) %all-to-all-start.4) | async-done | bytes 4194336 | tf_op jit(solution)/shard_map/all_to_all | solution.py:119
  792.1 8.8 %reshape.257 = bf16[2048,1,1024]{2,1,0:T(2,128)(2,1)} reshape(bf16[8,2,131072]{2,1,0:T(2,128)(2,1)} %all-to-all-done.4) | data formatting | bytes 8388608
  (348 shorter events, 375.4 us)
Async XLA Ops:
  10.1 21.8 %all-to-all-start = ((bf16[128,8,256]{2,0,1:T(8,128)(2,1)}), bf16[128,8,256]{2,0,1:T(8,128)(2,1)S(1)}, u32[]{:S(2)}, u32[]{:S(2)}) async-start(bf16[128,8,256]{2,0,1:T(8,128)(2,1)} %maximum_bitcast_fusion), calls=%async_computation | async-start | bytes 1048576 | tf_op jit(solution)/shard_map/all_to_all | solution.py:60
  31.9 8.4 %copy-start.6 = (bf16[128,8,256]{2,0,1:T(8,128)(2,1)}, bf16[128,8,256]{2,0,1:T(8,128)(2,1)S(1)}, u32[]{:S(2)}) copy-start(bf16[128,8,256]{2,0,1:T(8,128)(2,1)S(1)} %all-to-all-done) | copy-start | bytes 1572868
  31.9 52.1 %all-to-all-start.1 = ((bf16[128,8,1024]{2,0,1:T(8,128)(2,1)}), bf16[128,8,1024]{2,0,1:T(8,128)(2,1)S(1)}, u32[]{:S(2)}, u32[]{:S(2)}) async-start(bf16[128,8,1024]{2,0,1:T(8,128)(2,1)} %copy.131), calls=%async_computation.1 | async-start | bytes 4194304 | tf_op jit(solution)/shard_map/all_to_all | solution.py:59
  83.9 97.2 %all-to-all-start.3 = ((bf16[256,8,1024]{2,0,1:T(8,128)(2,1)}), bf16[256,8,1024]{2,0,1:T(8,128)(2,1)}, u32[]{:S(2)}, u32[]{:S(2)}) async-start(bf16[256,8,1024]{2,0,1:T(8,128)(2,1)} %bitcast.255), calls=%async_computation.3 | async-start | bytes 8388608 | tf_op jit(solution)/shard_map/all_to_all | solution.py:64
  88.6 97.8 %all-gather.2.cloned.1.call-start = ((), (), s32[]{:S(2)}) async-start(), calls=%async_computation.9 | async-start | bytes 2621440 | tf_op jit(solution)/shard_map/all_gather | solution.py:62
  103.4 82.9 %copy-start.9 = (s32[32]{0:T(128)S(1)}, s32[32]{0:T(128)}, u32[]{:S(2)}) copy-start(s32[32]{0:T(128)} %param.12) | copy-start | bytes 388
  181.2 53.0 %all-to-all-start.2 = ((bf16[4,4,128,1024]{2,3,1,0:T(8,128)(2,1)}), bf16[4,4,128,1024]{2,3,1,0:T(8,128)(2,1)}, u32[]{:S(2)}, u32[]{:S(2)}) async-start(bf16[4,4,128,1024]{2,3,1,0:T(8,128)(2,1)} %broadcast_select_fusion.3), calls=%async_computation.2 | async-start | bytes 8388608 | tf_op jit(solution)/shard_map/all_to_all | solution.py:75
  186.0 395.6 %reduce-scatter.2.cloned.1.call-start = ((), (), s32[]{:S(2)}) async-start(), calls=%async_computation.10 | async-start | bytes 2621440 | tf_op jit(solution)/shard_map/reduce_scatter | solution.py:134
  259.8 19.9 %copy-start.3 = (bf16[4,896,256]{2,1,0:T(8,128)(2,1)}, bf16[4,896,256]{2,1,0:T(8,128)(2,1)S(1)}, u32[]{:S(2)}) copy-start(bf16[4,896,256]{2,1,0:T(8,128)(2,1)S(1)} %get-tuple-element.411) | copy-start | bytes 5505028 | tf_op jit(solution)/shard_map/while
  297.9 5.9 copy-start
  297.9 10.5 %slice-start = ((s8[4980736]{0:T(1024)(128)(4,1)}), s8[4194304]{0:T(1024)(128)(4,1)S(1)}, s32[]{:S(2)}) async-start(s8[4980736]{0:T(1024)(128)(4,1)} %bitcast.249), calls=%async_computation.11 | async-start | bytes 8388608 | tf_op jit(solution)/shard_map/while
  334.5 19.9 %copy-start.3 = (bf16[4,896,256]{2,1,0:T(8,128)(2,1)}, bf16[4,896,256]{2,1,0:T(8,128)(2,1)S(1)}, u32[]{:S(2)}) copy-start(bf16[4,896,256]{2,1,0:T(8,128)(2,1)S(1)} %get-tuple-element.411) | copy-start | bytes 5505028 | tf_op jit(solution)/shard_map/while
  372.6 5.9 copy-start
  372.6 10.5 %slice-start = ((s8[4980736]{0:T(1024)(128)(4,1)}), s8[4194304]{0:T(1024)(128)(4,1)S(1)}, s32[]{:S(2)}) async-start(s8[4980736]{0:T(1024)(128)(4,1)} %bitcast.249), calls=%async_computation.11 | async-start | bytes 8388608 | tf_op jit(solution)/shard_map/while
  409.1 19.9 %copy-start.3 = (bf16[4,896,256]{2,1,0:T(8,128)(2,1)}, bf16[4,896,256]{2,1,0:T(8,128)(2,1)S(1)}, u32[]{:S(2)}) copy-start(bf16[4,896,256]{2,1,0:T(8,128)(2,1)S(1)} %get-tuple-element.411) | copy-start | bytes 5505028 | tf_op jit(solution)/shard_map/while
  447.3 10.5 %slice-start = ((s8[4980736]{0:T(1024)(128)(4,1)}), s8[4194304]{0:T(1024)(128)(4,1)S(1)}, s32[]{:S(2)}) async-start(s8[4980736]{0:T(1024)(128)(4,1)} %bitcast.249), calls=%async_computation.11 | async-start | bytes 8388608 | tf_op jit(solution)/shard_map/while
  483.8 19.9 %copy-start.3 = (bf16[4,896,256]{2,1,0:T(8,128)(2,1)}, bf16[4,896,256]{2,1,0:T(8,128)(2,1)S(1)}, u32[]{:S(2)}) copy-start(bf16[4,896,256]{2,1,0:T(8,128)(2,1)S(1)} %get-tuple-element.411) | copy-start | bytes 5505028 | tf_op jit(solution)/shard_map/while
  521.9 10.5 %slice-start = ((s8[4980736]{0:T(1024)(128)(4,1)}), s8[4194304]{0:T(1024)(128)(4,1)S(1)}, s32[]{:S(2)}) async-start(s8[4980736]{0:T(1024)(128)(4,1)} %bitcast.249), calls=%async_computation.11 | async-start | bytes 8388608 | tf_op jit(solution)/shard_map/while
  540.6 64.3 %all-to-all-start.5 = ((bf16[4,4,128,1024]{2,3,1,0:T(8,128)(2,1)}), bf16[4,4,128,1024]{2,3,1,0:T(8,128)(2,1)}, u32[]{:S(2)}, u32[]{:S(2)}) async-start(bf16[4,4,128,1024]{2,3,1,0:T(8,128)(2,1)} %bitcast.264), calls=%async_computation.5 | async-start | bytes 8388608 | tf_op jit(solution)/shard_map/all_to_all | solution.py:123
  604.9 25.6 %all-to-all-start.7 = ((bf16[8,2,16384]{2,1,0:T(2,128)(2,1)}), bf16[8,2,16384]{2,1,0:T(2,128)(2,1)S(1)}, u32[]{:S(2)}, u32[]{:S(2)}) async-start(bf16[8,2,16384]{2,1,0:T(2,128)(2,1)} %reshape.260), calls=%async_computation.8 | async-start | bytes 1048576 | tf_op jit(solution)/shard_map/all_to_all | solution.py:138
  608.5 6.6 copy-start.8
  630.5 29.8 %copy-start.5 = (bf16[8,2,16384]{2,1,0:T(2,128)(2,1)}, bf16[8,2,16384]{2,1,0:T(2,128)(2,1)S(1)}, u32[]{:S(2)}) copy-start(bf16[8,2,16384]{2,1,0:T(2,128)(2,1)S(1)} %all-to-all-done.7) | copy-start | bytes 1572868
  630.5 63.6 %all-to-all-start.6 = ((bf16[8,2,65536]{2,1,0:T(2,128)(2,1)}), bf16[8,2,65536]{2,1,0:T(2,128)(2,1)S(1)}, u32[]{:S(2)}, u32[]{:S(2)}) async-start(bf16[8,2,65536]{2,1,0:T(2,128)(2,1)} %reshape.258), calls=%async_computation.6 | async-start | bytes 4194304 | tf_op jit(solution)/shard_map/all_to_all | solution.py:131
  694.2 97.9 %all-to-all-start.4 = ((bf16[8,2,131072]{2,1,0:T(2,128)(2,1)}), bf16[8,2,131072]{2,1,0:T(2,128)(2,1)}, u32[]{:S(2)}, u32[]{:S(2)}) async-start(bf16[8,2,131072]{2,1,0:T(2,128)(2,1)} %reshape.256), calls=%async_computation.4 | async-start | bytes 8388608 | tf_op jit(solution)/shard_map/all_to_all | solution.py:119
  (19 other events, 76.2 us)
Sparse Core Ops, SparseCore 0:
  91.0 23.8 all-gather.1
  540.7 40.8 reduce-scatter.1
where the time goes:
time: 833 us; the launch traced here: 828 us
  waiting for transfers between devices  299 us (36%)
  local copies, waits for them, and re-layouts  230 us (28%)
  matrix products  144 us (17%)
  other arithmetic  85.5 us (10%)
  starting transfers between devices  41 us (5%)
  between operations  14.3 us (2%)
  loops' own time  13.8 us (2%)
    all_to_all x1, waiting for transfers between devices, body(): lax.all_to_all(grad_split, 'head', split_axis=1, concat_axis=0, tiled=True)  77.7 us
    all_to_all x1, waiting for transfers between devices, body(): lax.all_to_all(out_slots, 'head', split_axis=0, concat_axis=1, tiled=True)  73.7 us
    unnamed x27, local copies, waits for them, and re-layouts  60.6 us
    gather x96, local copies, waits for them, and re-layouts  59.3 us
    all_to_all x1, waiting for transfers between devices, body(): lax.all_to_all(query_split, 'head', split_axis=1, concat_axis=0, tiled=True)  43.6 us
    sub x4, matrix products, slot_pass(): scores - rowmax  39.8 us
    convert_element_type x4, other arithmetic, slot_pass(): weights_b = weights.astype(jnp.bfloat16)  39.7 us
    all_to_all x1, waiting for transfers between devices, body(): lax.all_to_all(outgoing, 'seq', split_axis=0, concat_axis=0, tiled=True)  39.3 us
  transfers between devices with their start and end apart: 10, of which 7 were waited for; matrix products, arithmetic and copies ran while one was open for 16% of the time, Pallas kernels for 0%

commit v1 on v0

--- a/solution.py
+++ b/solution.py
@@ -9,6 +9,22 @@
 DH = 128
 BLOCK = 128
 DOCMAX = 7
+
+
+def pairwise_exchange(array, axis, split, join):
+    ways, here = (lax.axis_size(axis), lax.axis_index(axis))
+    width = array.shape[split] // ways
+    dims = list(array.shape)
+    dims[split] = width
+    height = dims[join]
+    dims[join] = height * ways
+    full = jnp.zeros(dims, array.dtype)
+    for mask in range(ways):
+        part = lax.dynamic_slice_in_dim(array, (here ^ mask) * width, width, axis=split)
+        if mask:
+            part = lax.ppermute(part, axis, [(d, d ^ mask) for d in range(ways)])
+        full = lax.dynamic_update_slice_in_dim(full, part, (here ^ mask) * height, axis=join)
+    return full
 
 
 def slot_pass(queries, cotangent, keys_win, values_win, allowed, alive_flag, factor):
@@ -116,9 +132,7 @@
         group_step, partial_init, jnp.arange(group_count)
     )
     out_slots = outputs.reshape(slot_total * BLOCK, 1, per_dev * DH)
-    attn_out = lax.all_to_all(out_slots, "head", split_axis=0, concat_axis=1, tiled=True).reshape(
-        2 * tok_count, QH * DH
-    )
+    attn_out = pairwise_exchange(out_slots, "head", 0, 1).reshape(2 * tok_count, QH * DH)
     back_slots = grad_rows.reshape(seq_count, slot_cap, BLOCK, per_dev * DH)
     returned = lax.all_to_all(back_slots, "seq", split_axis=0, concat_axis=0, tiled=True).reshape(
         slot_total, BLOCK, per_dev * DH

time: 833 us -> 860 us (1.032); the launches traced: 828 us -> 844 us
  starting transfers between devices: 41 us -> 53.4 us
  other arithmetic: 85.5 us -> 94.7 us
    ppermute x0 -> x7, waiting for transfers between devices: none -> 79 us  [pairwise_exchange(): part = lax.ppermute(part, axis, [(d, d ^ mask) for d in range(ways)])]
    all_to_all x1 -> x0, waiting for transfers between devices: 73.7 us -> none  [body(): lax.all_to_all(out_slots, 'head', split_axis=0, concat_axis=1, tiled=True)]
    dynamic_update_slice x16, other arithmetic: 2.86 us -> 38 us  [group_step(): lax.dynamic_update_slice_in_dim(partial_value, current + updates[member],...]
    dynamic_update_slice x0 -> x8, local copies, waits for them, and re-layouts: none -> 34.1 us  [pairwise_exchange(): lax.dynamic_update_slice_in_dim(full, part, (here ^ mask) * height, axis=...]
    reshape x1 -> x0, other arithmetic: 26 us -> none  [body(): out_slots = outputs.reshape(slot_total * BLOCK, 1, per_dev * DH)]
    unnamed x27 -> x26, local copies, waits for them, and re-layouts: 60.6 us -> 40.2 us
    ppermute x0 -> x7, starting transfers between devices: none -> 18.4 us  [pairwise_exchange(): part = lax.ppermute(part, axis, [(d, d ^ mask) for d in range(ways)])]
    reshape x2 -> x1, local copies, waits for them, and re-layouts: 24.3 us -> 7.28 us  [body(): out_slots = outputs.reshape(slot_total * BLOCK, 1, per_dev * DH)]
  transfers between devices with their start and end apart: 10 -> 16, of which waited for: 7 -> 11; matrix products, arithmetic and copies ran while one was open for 16% -> 14% of each run, Pallas kernels for 0% -> 0%
where the time goes in v1:
time: 860 us; the launch traced here: 844 us
  waiting for transfers between devices  304 us (35%)
  local copies, waits for them, and re-layouts  225 us (26%)
  matrix products  139 us (16%)
  other arithmetic  94.7 us (11%)
  starting transfers between devices  53.4 us (6%)
  between operations  14.3 us (2%)
  loops' own time  13.5 us (2%)
    ppermute x7, waiting for transfers between devices, pairwise_exchange(): part = lax.ppermute(part, axis, [(d, d ^ mask) for d in range(ways)])  79 us
    all_to_all x1, waiting for transfers between devices, body(): lax.all_to_all(grad_split, 'head', split_axis=1, concat_axis=0, tiled=True)  77.7 us
    gather x96, local copies, waits for them, and re-layouts  59.6 us
    all_to_all x1, waiting for transfers between devices, body(): lax.all_to_all(query_split, 'head', split_axis=1, concat_axis=0, tiled=True)  43.6 us
    unnamed x26, local copies, waits for them, and re-layouts  40.2 us
    sub x4, matrix products, slot_pass(): scores - rowmax  40 us
    convert_element_type x4, other arithmetic, slot_pass(): weights_b = weights.astype(jnp.bfloat16)  39.8 us
    all_to_all x1, waiting for transfers between devices, body(): lax.all_to_all(outgoing, 'seq', split_axis=0, concat_axis=0, tiled=True)  39.3 us
  transfers between devices with their start and end apart: 16, of which 11 were waited for; matrix products, arithmetic and copies ran while one was open for 14% of the time, Pallas kernels for 0%

profile of v1, /device:TPU:0, one launch (start us, length us, event | category | flops | bytes accessed | tf_op | source)
XLA Modules:
  0.0 844.1 jit_solution(11111543176440085091)
XLA Ops:
  23.2 8.7 %all-to-all-done = bf16[128,8,256]{2,0,1:T(8,128)(2,1)S(1)} async-done(((bf16[128,8,256]{2,0,1:T(8,128)(2,1)}), bf16[128,8,256]{2,0,1:T(8,128)(2,1)S(1)}, u32[]{:S(2)}, u32[]{:S(2)}) %all-to-all-start) | async-done | bytes 524320 | tf_op jit(solution)/shard_map/all_to_all | solution.py:76
  40.3 43.6 %all-to-all-done.1 = bf16[128,8,1024]{2,0,1:T(8,128)(2,1)S(1)} async-done(((bf16[128,8,1024]{2,0,1:T(8,128)(2,1)}), bf16[128,8,1024]{2,0,1:T(8,128)(2,1)S(1)}, u32[]{:S(2)}, u32[]{:S(2)}) %all-to-all-start.1) | async-done | bytes 2097184 | tf_op jit(solution)/shard_map/all_to_all | solution.py:75
  103.5 77.7 %all-to-all-done.3 = bf16[256,8,1024]{2,0,1:T(8,128)(2,1)} async-done(((bf16[256,8,1024]{2,0,1:T(8,128)(2,1)}), bf16[256,8,1024]{2,0,1:T(8,128)(2,1)}, u32[]{:S(2)}, u32[]{:S(2)}) %all-to-all-start.3) | async-done | bytes 4194336 | tf_op jit(solution)/shard_map/all_to_all | solution.py:80
  194.9 39.3 %all-to-all-done.2 = bf16[4,4,128,1024]{2,3,1,0:T(8,128)(2,1)} async-done(((bf16[4,4,128,1024]{2,3,1,0:T(8,128)(2,1)}), bf16[4,4,128,1024]{2,3,1,0:T(8,128)(2,1)}, u32[]{:S(2)}, u32[]{:S(2)}) %all-to-all-start.2) | async-done | bytes 4194336 | tf_op jit(solution)/shard_map/all_to_all | solution.py:91
  236.8 327.1 %while.23 = (s32[]{:T(128)}, f32[4864,256]{0,1:T(8,128)}, bf16[4,4,128,8,128]{4,3,2,1,0:T(8,128)(2,1)}, bf16[4,4,128,8,128]{2,4,3,1,0:T(8,128)(2,1)}, s32[4]{0:T...) while((s32[]{:T(128)}, f32[4864,256]{0,1:T(8,128)}, ...), condition=%wide.region_4.5_spmd.clone, body=%wide.region_0.0_spmd.clone.sunk | while | flops 5688947712 | bytes 213390656 | solution.py:131
  248.4 9.6 %while.25 = (s32[]{:T(128)}, bf16[4864,256]{1,0:T(8,128)(2,1)}, s32[4,2]{0,1:T(2,128)S(1)}, bf16[4,896,256]{2,1,0:T(8,128)(2,1)S(1)}, s32[]{:T(128)}) while((s32[]{:T(128)}, bf16[4864,256]{1,0:T(8,128)(2,1)}, s32[4,2]{0,1:T(2,128)S(1)}, bf16[4,896,256]{2,1,0:T(8,128)(2,1)S(1)}, s32[]{:T(128)}) %tuple.93), condition=%wide.while_cond.1, body=%wide.while_body.1.sunk | while | flops 2 | bytes 917609 | solution.py:107
  258.0 10.0 %fusion.114 = (f32[4,8,128]{2,1,0:T(8,128)S(1)}, f32[4,8,128,896]{2,3,1,0:T(8,128)}) fusion(pred[4,128,896]{1,2,0:T(8,128)(4,1)S(1)} %broadcast_and_fusion.2, bf16[16,128,8,128]{1,3,2,0:T(8,128)(2,1)} %get-tuple-element.521, s32[]{:T(128)S(6)} %select_n.261, bf16[4,896,256]{2,1,0:T(8,128)(2,1)S(1)} %get-tuple-element.419), kind=kOutput, calls=%fused_computation.120.clone.1 | convolution fusion | flops 957875072 | bytes 17580036 | tf_op jit(solution)/shard_map/while/body/eval_jaxpr/vmap()/sub | solution.py:36
  268.0 9.9 %fusion.115 = bf16[4,8,128,896]{2,3,1,0:T(8,128)(2,1)} fusion(f32[4,8,128,896]{2,3,1,0:T(8,128)} %get-tuple-element.420, f32[4,8,128]{2,1,0:T(8,128)S(1)} %get-tuple-element.421), kind=kLoop, calls=%fused_computation.19.clone.1 | loop fusion | flops 7340032 | bytes 22036480 | tf_op jit(solution)/shard_map/while/body/eval_jaxpr/vmap()/convert_element_type | solution.py:38
  330.1 9.6 %while.25 = (s32[]{:T(128)}, bf16[4864,256]{1,0:T(8,128)(2,1)}, s32[4,2]{0,1:T(2,128)S(1)}, bf16[4,896,256]{2,1,0:T(8,128)(2,1)S(1)}, s32[]{:T(128)}) while((s32[]{:T(128)}, bf16[4864,256]{1,0:T(8,128)(2,1)}, s32[4,2]{0,1:T(2,128)S(1)}, bf16[4,896,256]{2,1,0:T(8,128)(2,1)S(1)}, s32[]{:T(128)}) %tuple.93), condition=%wide.while_cond.1, body=%wide.while_body.1.sunk | while | flops 2 | bytes 917609 | solution.py:107
  339.7 10.0 %fusion.114 = (f32[4,8,128]{2,1,0:T(8,128)S(1)}, f32[4,8,128,896]{2,3,1,0:T(8,128)}) fusion(pred[4,128,896]{1,2,0:T(8,128)(4,1)S(1)} %broadcast_and_fusion.2, bf16[16,128,8,128]{1,3,2,0:T(8,128)(2,1)} %get-tuple-element.521, s32[]{:T(128)S(6)} %select_n.261, bf16[4,896,256]{2,1,0:T(8,128)(2,1)S(1)} %get-tuple-element.419), kind=kOutput, calls=%fused_computation.120.clone.1 | convolution fusion | flops 957875072 | bytes 17580036 | tf_op jit(solution)/shard_map/while/body/eval_jaxpr/vmap()/sub | solution.py:36
  349.7 9.9 %fusion.115 = bf16[4,8,128,896]{2,3,1,0:T(8,128)(2,1)} fusion(f32[4,8,128,896]{2,3,1,0:T(8,128)} %get-tuple-element.420, f32[4,8,128]{2,1,0:T(8,128)S(1)} %get-tuple-element.421), kind=kLoop, calls=%fused_computation.19.clone.1 | loop fusion | flops 7340032 | bytes 22036480 | tf_op jit(solution)/shard_map/while/body/eval_jaxpr/vmap()/convert_element_type | solution.py:38
  411.9 9.6 %while.25 = (s32[]{:T(128)}, bf16[4864,256]{1,0:T(8,128)(2,1)}, s32[4,2]{0,1:T(2,128)S(1)}, bf16[4,896,256]{2,1,0:T(8,128)(2,1)S(1)}, s32[]{:T(128)}) while((s32[]{:T(128)}, bf16[4864,256]{1,0:T(8,128)(2,1)}, s32[4,2]{0,1:T(2,128)S(1)}, bf16[4,896,256]{2,1,0:T(8,128)(2,1)S(1)}, s32[]{:T(128)}) %tuple.93), condition=%wide.while_cond.1, body=%wide.while_body.1.sunk | while | flops 2 | bytes 917609 | solution.py:107
  421.5 10.0 %fusion.114 = (f32[4,8,128]{2,1,0:T(8,128)S(1)}, f32[4,8,128,896]{2,3,1,0:T(8,128)}) fusion(pred[4,128,896]{1,2,0:T(8,128)(4,1)S(1)} %broadcast_and_fusion.2, bf16[16,128,8,128]{1,3,2,0:T(8,128)(2,1)} %get-tuple-element.521, s32[]{:T(128)S(6)} %select_n.261, bf16[4,896,256]{2,1,0:T(8,128)(2,1)S(1)} %get-tuple-element.419), kind=kOutput, calls=%fused_computation.120.clone.1 | convolution fusion | flops 957875072 | bytes 17580036 | tf_op jit(solution)/shard_map/while/body/eval_jaxpr/vmap()/sub | solution.py:36
  431.5 9.9 %fusion.115 = bf16[4,8,128,896]{2,3,1,0:T(8,128)(2,1)} fusion(f32[4,8,128,896]{2,3,1,0:T(8,128)} %get-tuple-element.420, f32[4,8,128]{2,1,0:T(8,128)S(1)} %get-tuple-element.421), kind=kLoop, calls=%fused_computation.19.clone.1 | loop fusion | flops 7340032 | bytes 22036480 | tf_op jit(solution)/shard_map/while/body/eval_jaxpr/vmap()/convert_element_type | solution.py:38
  493.7 9.6 %while.25 = (s32[]{:T(128)}, bf16[4864,256]{1,0:T(8,128)(2,1)}, s32[4,2]{0,1:T(2,128)S(1)}, bf16[4,896,256]{2,1,0:T(8,128)(2,1)S(1)}, s32[]{:T(128)}) while((s32[]{:T(128)}, bf16[4864,256]{1,0:T(8,128)(2,1)}, s32[4,2]{0,1:T(2,128)S(1)}, bf16[4,896,256]{2,1,0:T(8,128)(2,1)S(1)}, s32[]{:T(128)}) %tuple.93), condition=%wide.while_cond.1, body=%wide.while_body.1.sunk | while | flops 2 | bytes 917609 | solution.py:107
  503.3 10.0 %fusion.114 = (f32[4,8,128]{2,1,0:T(8,128)S(1)}, f32[4,8,128,896]{2,3,1,0:T(8,128)}) fusion(pred[4,128,896]{1,2,0:T(8,128)(4,1)S(1)} %broadcast_and_fusion.2, bf16[16,128,8,128]{1,3,2,0:T(8,128)(2,1)} %get-tuple-element.521, s32[]{:T(128)S(6)} %select_n.261, bf16[4,896,256]{2,1,0:T(8,128)(2,1)S(1)} %get-tuple-element.419), kind=kOutput, calls=%fused_computation.120.clone.1 | convolution fusion | flops 957875072 | bytes 17580036 | tf_op jit(solution)/shard_map/while/body/eval_jaxpr/vmap()/sub | solution.py:36
  513.3 9.9 %fusion.115 = bf16[4,8,128,896]{2,3,1,0:T(8,128)(2,1)} fusion(f32[4,8,128,896]{2,3,1,0:T(8,128)} %get-tuple-element.420, f32[4,8,128]{2,1,0:T(8,128)S(1)} %get-tuple-element.421), kind=kLoop, calls=%fused_computation.19.clone.1 | loop fusion | flops 7340032 | bytes 22036480 | tf_op jit(solution)/shard_map/while/body/eval_jaxpr/vmap()/convert_element_type | solution.py:38
  574.0 36.1 %reduce-scatter.2.cloned.1.call-done = bf16[1024,256]{1,0:T(8,128)(2,1)} async-done(((bf16[4096,256]{1,0:T(8,128)(2,1)}), bf16[1024,256]{1,0:T(8,128)(2,1)}) %reduce-scatter.2.cloned.1.call-update) | async-done | bytes 524304 | tf_op jit(solution)/shard_map/reduce_scatter | solution.py:148
  613.6 19.8 %all-to-all-done.4 = bf16[4,4,128,1024]{2,3,1,0:T(8,128)(2,1)} async-done(((bf16[4,4,128,1024]{2,3,1,0:T(8,128)(2,1)}), bf16[4,4,128,1024]{2,3,1,0:T(8,128)(2,1)}, u32[]{:S(2)}, u32[]{:S(2)}) %all-to-all-start.4) | async-done | bytes 4194336 | tf_op jit(solution)/shard_map/all_to_all | solution.py:137
  685.9 16.0 %collective-permute-done = bf16[256,1,1024]{2,0,1:T(8,128)(2,1)} collective-permute-done((bf16[256,1,1024]{2,0,1:T(8,128)(2,1)}, bf16[256,1,1024]{2,0,1:T(8,128)(2,1)}, u32[]{:S(2)}, u32[]{:S(2)}) %collective-permute-start) | collective-permute-done | bytes 524320 | tf_op jit(solution)/shard_map/ppermute | solution.py:25
  711.0 13.9 %collective-permute-done.1 = bf16[256,1,1024]{2,0,1:T(8,128)(2,1)} collective-permute-done((bf16[256,1,1024]{2,0,1:T(8,128)(2,1)}, bf16[256,1,1024]{2,0,1:T(8,128)(2,1)}, u32[]{:S(2)}, u32[]{:S(2)}) %collective-permute-start.1) | collective-permute-done | bytes 524320 | tf_op jit(solution)/shard_map/ppermute | solution.py:25
  738.0 32.9 %collective-permute-done.3 = bf16[256,1,1024]{2,0,1:T(8,128)(2,1)S(1)} collective-permute-done((bf16[256,1,1024]{2,0,1:T(8,128)(2,1)}, bf16[256,1,1024]{2,0,1:T(8,128)(2,1)S(1)}, u32[]{:S(2)}, u32[]{:S(2)}) %collective-permute-start.3) | collective-permute-done | bytes 524320 | tf_op jit(solution)/shard_map/ppermute | solution.py:25
  771.7 10.2 %collective-permute-done.4 = bf16[256,1,1024]{2,0,1:T(8,128)(2,1)S(1)} collective-permute-done((bf16[256,1,1024]{2,0,1:T(8,128)(2,1)}, bf16[256,1,1024]{2,0,1:T(8,128)(2,1)S(1)}, u32[]{:S(2)}, u32[]{:S(2)}) %collective-permute-start.4) | collective-permute-done | bytes 524320 | tf_op jit(solution)/shard_map/ppermute | solution.py:25
  790.7 19.6 %dynamic_update_slice.50 = bf16[256,8,1024]{2,1,0:T(8,128)(2,1)} dynamic-update-slice(bf16[256,8,1024]{2,1,0:T(8,128)(2,1)} %copy.137, bf16[256,1,1024]{2,1,0:T(2,128)(2,1)S(1)} %copy.138, s32[]{:T(128)} %constant.47.clone.1, s32[]{:T(128)S(6)} %select_n.185, s32[]{:T(128)} %constant.47.clone.1) | dynamic-update-slice | bytes 1048580 | tf_op jit(solution)/shard_map/dynamic_update_slice | solution.py:26
  (348 shorter events, 440.6 us)
Async XLA Ops:
  10.1 21.8 %all-to-all-start = ((bf16[128,8,256]{2,0,1:T(8,128)(2,1)}), bf16[128,8,256]{2,0,1:T(8,128)(2,1)S(1)}, u32[]{:S(2)}, u32[]{:S(2)}) async-start(bf16[128,8,256]{2,0,1:T(8,128)(2,1)} %maximum_bitcast_fusion), calls=%async_computation | async-start | bytes 1048576 | tf_op jit(solution)/shard_map/all_to_all | solution.py:76
  31.9 8.5 %copy-start.7 = (bf16[128,8,256]{2,0,1:T(8,128)(2,1)}, bf16[128,8,256]{2,0,1:T(8,128)(2,1)S(1)}, u32[]{:S(2)}) copy-start(bf16[128,8,256]{2,0,1:T(8,128)(2,1)S(1)} %all-to-all-done) | copy-start | bytes 1572868
  31.9 52.1 %all-to-all-start.1 = ((bf16[128,8,1024]{2,0,1:T(8,128)(2,1)}), bf16[128,8,1024]{2,0,1:T(8,128)(2,1)S(1)}, u32[]{:S(2)}, u32[]{:S(2)}) async-start(bf16[128,8,1024]{2,0,1:T(8,128)(2,1)} %copy.131), calls=%async_computation.1 | async-start | bytes 4194304 | tf_op jit(solution)/shard_map/all_to_all | solution.py:75
  83.9 97.2 %all-to-all-start.3 = ((bf16[256,8,1024]{2,0,1:T(8,128)(2,1)}), bf16[256,8,1024]{2,0,1:T(8,128)(2,1)}, u32[]{:S(2)}, u32[]{:S(2)}) async-start(bf16[256,8,1024]{2,0,1:T(8,128)(2,1)} %bitcast.249), calls=%async_computation.3 | async-start | bytes 8388608 | tf_op jit(solution)/shard_map/all_to_all | solution.py:80
  88.6 97.8 %all-gather.2.cloned.1.call-start = ((), (), s32[]{:S(2)}) async-start(), calls=%async_computation.8 | async-start | bytes 2621440 | tf_op jit(solution)/shard_map/all_gather | solution.py:78
  103.5 82.8 %copy-start.10 = (s32[32]{0:T(128)S(1)}, s32[32]{0:T(128)}, u32[]{:S(2)}) copy-start(s32[32]{0:T(128)} %param.12) | copy-start | bytes 388
  181.2 53.1 %all-to-all-start.2 = ((bf16[4,4,128,1024]{2,3,1,0:T(8,128)(2,1)}), bf16[4,4,128,1024]{2,3,1,0:T(8,128)(2,1)}, u32[]{:S(2)}, u32[]{:S(2)}) async-start(bf16[4,4,128,1024]{2,3,1,0:T(8,128)(2,1)} %broadcast_select_fusion.3), calls=%async_computation.2 | async-start | bytes 8388608 | tf_op jit(solution)/shard_map/all_to_all | solution.py:91
  186.0 424.0 %reduce-scatter.2.cloned.1.call-start = ((), (), s32[]{:S(2)}) async-start(), calls=%async_computation.9 | async-start | bytes 2621440 | tf_op jit(solution)/shard_map/reduce_scatter | solution.py:148
  258.0 25.4 %copy-start.5 = (bf16[4,896,256]{2,1,0:T(8,128)(2,1)}, bf16[4,896,256]{2,1,0:T(8,128)(2,1)S(1)}, u32[]{:S(2)}) copy-start(bf16[4,896,256]{2,1,0:T(8,128)(2,1)S(1)} %get-tuple-element.419) | copy-start | bytes 5505028 | tf_op jit(solution)/shard_map/while
  339.7 25.4 %copy-start.5 = (bf16[4,896,256]{2,1,0:T(8,128)(2,1)}, bf16[4,896,256]{2,1,0:T(8,128)(2,1)S(1)}, u32[]{:S(2)}) copy-start(bf16[4,896,256]{2,1,0:T(8,128)(2,1)S(1)} %get-tuple-element.419) | copy-start | bytes 5505028 | tf_op jit(solution)/shard_map/while
  421.5 25.4 %copy-start.5 = (bf16[4,896,256]{2,1,0:T(8,128)(2,1)}, bf16[4,896,256]{2,1,0:T(8,128)(2,1)S(1)}, u32[]{:S(2)}) copy-start(bf16[4,896,256]{2,1,0:T(8,128)(2,1)S(1)} %get-tuple-element.419) | copy-start | bytes 5505028 | tf_op jit(solution)/shard_map/while
  503.3 25.4 %copy-start.5 = (bf16[4,896,256]{2,1,0:T(8,128)(2,1)}, bf16[4,896,256]{2,1,0:T(8,128)(2,1)S(1)}, u32[]{:S(2)}) copy-start(bf16[4,896,256]{2,1,0:T(8,128)(2,1)S(1)} %get-tuple-element.419) | copy-start | bytes 5505028 | tf_op jit(solution)/shard_map/while
  569.1 64.3 %all-to-all-start.4 = ((bf16[4,4,128,1024]{2,3,1,0:T(8,128)(2,1)}), bf16[4,4,128,1024]{2,3,1,0:T(8,128)(2,1)}, u32[]{:S(2)}, u32[]{:S(2)}) async-start(bf16[4,4,128,1024]{2,3,1,0:T(8,128)(2,1)} %bitcast.258), calls=%async_computation.4 | async-start | bytes 8388608 | tf_op jit(solution)/shard_map/all_to_all | solution.py:137
  633.4 25.6 %all-to-all-start.6 = ((bf16[8,2,16384]{2,1,0:T(2,128)(2,1)}), bf16[8,2,16384]{2,1,0:T(2,128)(2,1)S(1)}, u32[]{:S(2)}, u32[]{:S(2)}) async-start(bf16[8,2,16384]{2,1,0:T(2,128)(2,1)} %reshape.256), calls=%async_computation.7 | async-start | bytes 1048576 | tf_op jit(solution)/shard_map/all_to_all | solution.py:152
  637.0 6.6 copy-start.9
  659.0 13.3 %copy-start.6 = (bf16[8,2,16384]{2,1,0:T(2,128)(2,1)}, bf16[8,2,16384]{2,1,0:T(2,128)(2,1)S(1)}, u32[]{:S(2)}) copy-start(bf16[8,2,16384]{2,1,0:T(2,128)(2,1)S(1)} %all-to-all-done.6) | copy-start | bytes 1572868
  659.0 164.4 %all-to-all-start.5 = ((bf16[8,2,65536]{2,1,0:T(2,128)(2,1)}), bf16[8,2,65536]{2,1,0:T(2,128)(2,1)S(1)}, u32[]{:S(2)}, u32[]{:S(2)}) async-start(bf16[8,2,65536]{2,1,0:T(2,128)(2,1)} %reshape.254), calls=%async_computation.5 | async-start | bytes 4194304 | tf_op jit(solution)/shard_map/all_to_all | solution.py:145
  678.0 23.8 %collective-permute-start = (bf16[256,1,1024]{2,0,1:T(8,128)(2,1)}, bf16[256,1,1024]{2,0,1:T(8,128)(2,1)}, u32[]{:S(2)}, u32[]{:S(2)}) collective-permute-start(bf16[256,1,1024]{2,0,1:T(8,128)(2,1)} %get-tuple-element.260), channel_id=1, source_target_pairs={{0,1},{1,0},{2,3},{3,2},{4,5},{5,4},{6,7},{7,6},{8,9},{9,8},{10,11... | collective-permute-start | bytes 1572872 | tf_op jit(solution)/shard_map/ppermute | solution.py:25
  680.1 44.8 %collective-permute-start.1 = (bf16[256,1,1024]{2,0,1:T(8,128)(2,1)}, bf16[256,1,1024]{2,0,1:T(8,128)(2,1)}, u32[]{:S(2)}, u32[]{:S(2)}) collective-permute-start(bf16[256,1,1024]{2,0,1:T(8,128)(2,1)} %get-tuple-element.259), channel_id=1, source_target_pairs={{0,2},{1,3},{2,0},{3,1},{4,6},{5,7},{6,4},{7,5},{8,10},{9,11},{10,... | collective-permute-start | bytes 1572872 | tf_op jit(solution)/shard_map/ppermute | solution.py:25
  681.5 54.6 %collective-permute-start.2 = (bf16[256,1,1024]{2,0,1:T(8,128)(2,1)}, bf16[256,1,1024]{2,0,1:T(8,128)(2,1)}, u32[]{:S(2)}, u32[]{:S(2)}) collective-permute-start(bf16[256,1,1024]{2,0,1:T(8,128)(2,1)} %get-tuple-element.258), channel_id=1, source_target_pairs={{0,3},{1,2},{2,1},{3,0},{4,7},{5,6},{6,5},{7,4},{8,11},{9,10},{10,... | collective-permute-start | bytes 1572872 | tf_op jit(solution)/shard_map/ppermute | solution.py:25
  681.5 89.3 %collective-permute-start.3 = (bf16[256,1,1024]{2,0,1:T(8,128)(2,1)}, bf16[256,1,1024]{2,0,1:T(8,128)(2,1)S(1)}, u32[]{:S(2)}, u32[]{:S(2)}) collective-permute-start(bf16[256,1,1024]{2,0,1:T(8,128)(2,1)} %get-tuple-element.257), channel_id=1, source_target_pairs={{0,4},{1,5},{2,6},{3,7},{4,0},{5,1},{6,2},{7,3},{8,12},{9,13},{10,... | collective-permute-start | bytes 1572872 | tf_op jit(solution)/shard_map/ppermute | solution.py:25
  684.5 97.4 %collective-permute-start.4 = (bf16[256,1,1024]{2,0,1:T(8,128)(2,1)}, bf16[256,1,1024]{2,0,1:T(8,128)(2,1)S(1)}, u32[]{:S(2)}, u32[]{:S(2)}) collective-permute-start(bf16[256,1,1024]{2,0,1:T(8,128)(2,1)} %get-tuple-element.256), channel_id=1, source_target_pairs={{0,5},{1,4},{2,7},{3,6},{4,1},{5,0},{6,3},{7,2},{8,13},{9,12},{10,... | collective-permute-start | bytes 1572872 | tf_op jit(solution)/shard_map/ppermute | solution.py:25
  701.9 80.8 %collective-permute-start.5 = (bf16[256,1,1024]{2,0,1:T(8,128)(2,1)}, bf16[256,1,1024]{2,0,1:T(8,128)(2,1)S(1)}, u32[]{:S(2)}, u32[]{:S(2)}) collective-permute-start(bf16[256,1,1024]{2,0,1:T(8,128)(2,1)} %get-tuple-element.255), channel_id=1, source_target_pairs={{0,6},{1,7},{2,4},{3,5},{4,2},{5,3},{6,0},{7,1},{8,14},{9,15},{10,... | collective-permute-start | bytes 1572872 | tf_op jit(solution)/shard_map/ppermute | solution.py:25
  724.9 65.0 %collective-permute-start.6 = (bf16[256,1,1024]{2,0,1:T(8,128)(2,1)}, bf16[256,1,1024]{2,0,1:T(8,128)(2,1)S(1)}, u32[]{:S(2)}, u32[]{:S(2)}) collective-permute-start(bf16[256,1,1024]{2,0,1:T(8,128)(2,1)} %get-tuple-element.254), channel_id=1, source_target_pairs={{0,7},{1,6},{2,5},{3,4},{4,3},{5,2},{6,1},{7,0},{8,15},{9,14},{10,... | collective-permute-start | bytes 1572872 | tf_op jit(solution)/shard_map/ppermute | solution.py:25
  (18 other events, 78.2 us)
Sparse Core Ops, SparseCore 0:
  91.0 23.8 all-gather.1
  569.2 40.8 reduce-scatter.1
